TPU v7x, 512 devices: a whole 4x8x8 slice. The times are simulated.
512 devices in a mesh: section: 4 (over x), sub: 32 (over z_lo, y), rng: 4 (over z_hi, core).
Axes of the slice: x: 4, y: 8, z: 8 (z_hi: 2, z_lo: 4; z = z_hi * 4 + z_lo), core: 2. Of those that a mesh axis runs over, the one named last changes fastest.
Arguments:
- echoes: bfloat16 [2, 32, 24, 16384], P(None, 'sub', 'section', 'rng'), may hold values from -6 to 6
- chirp: bfloat16 [2, 2048], replicated, may hold values from -0.25 to 0.25
- steer: bfloat16 [2, 32, 128, 24], P(None, 'sub'), may hold values from -2 to 2
- pulse_order: int32 [32, 24], P('sub'), may hold values from 0 to 23, each once within a row
- band_coef: bfloat16 [5, 32, 2, 2, 128, 16], P(None, 'sub'), may hold values from -2.5 to 2.5
- band_start: int32 [5, 32, 2, 128], P(None, 'sub'), may hold values from 0 to 112
- band_width: int32 [5, 32, 2, 128], P(None, 'sub'), may hold values from 1 to 16
Outputs:
- image: bfloat16 [2, 4096, 4, 4096], P(None, 'sub', 'rng', 'section')
Inputs may be any that keep to these rules, and one draw needn't show every extreme that they name: `pulse_order`: each row is a permutation of the 24 aperture positions.
All inputs are finite; a program needn't handle non-finite values.
Results may differ from a plain program's by a relative error of at most 0.0085.
Values may be sent and summed in bfloat16 or wider, within the bound.
A program may use at most 64 MiB of HBM per device.

v0:
```python
import jax
import jax.numpy as jnp
from jax import lax
from jax.sharding import PartitionSpec as P

CBLK = 128


def from_behind(value, axis, by):
    size = lax.axis_size(axis)
    pairs = [(i, i + by) for i in range(size) if 0 <= i + by < size]
    return lax.ppermute(value, axis, pairs)


def from_partner(block, axis, stride):
    count = lax.axis_size(axis)
    route = []
    for low in range(count):
        high = low | 1 << stride
        if high != low and high < count:
            route += [(low, high), (high, low)]
    return lax.ppermute(block, axis, route)


def band_matrix(coef_side, start_side, width_side):
    beam_count = coef_side.shape[1]
    tap_count = coef_side.shape[2]
    column = jnp.arange(beam_count, dtype=jnp.int32)
    offset = column[None, :] - start_side[:, None]
    taps = jnp.arange(tap_count, dtype=jnp.int32)
    hits = (offset[None, :, :] == taps[:, None, None]) & (
        taps[:, None, None] < width_side[None, :, None]
    )
    selector = hits.astype(jnp.bfloat16)
    return jnp.einsum(
        "sqt,tqc->sqc", coef_side, selector, preferred_element_type=jnp.float32
    ).astype(jnp.bfloat16)


def merge_level(own, partner_image, coef_level, start_level, width_level):
    self_matrix = band_matrix(coef_level[0], start_level[0], width_level[0])
    cross_matrix = band_matrix(coef_level[1], start_level[1], width_level[1])
    upper_rows = jnp.concatenate(
        [self_matrix[0], -self_matrix[1], cross_matrix[0], -cross_matrix[1]], axis=1
    )
    lower_rows = jnp.concatenate(
        [self_matrix[1], self_matrix[0], cross_matrix[1], cross_matrix[0]], axis=1
    )
    operator = jnp.concatenate([upper_rows, lower_rows], axis=0)
    stacked = jnp.concatenate([own[0], own[1], partner_image[0], partner_image[1]], axis=0)
    merged = jnp.dot(operator, stacked, preferred_element_type=jnp.float32)
    return merged.reshape(2, own.shape[1], own.shape[2]).astype(jnp.bfloat16)


def lag_tables(chirp, extra_blocks):
    tap_count = chirp.shape[1]
    padded = jnp.concatenate(
        [jnp.zeros((2, CBLK), jnp.bfloat16), chirp, jnp.zeros((2, 2 * CBLK), jnp.bfloat16)], axis=1
    )
    total_len = tap_count + 3 * CBLK
    tiled = jnp.tile(padded, (1, CBLK))[:, : CBLK * (total_len - 1)]
    shifted = tiled.reshape(2, CBLK, total_len - 1)[:, :, CBLK : CBLK + (extra_blocks + 1) * CBLK]
    shifted = shifted.reshape(2, CBLK, extra_blocks + 1, CBLK)
    return jnp.transpose(shifted, (0, 2, 3, 1))


def compress(signal, chirp):
    pulse_count = signal.shape[1]
    range_count = signal.shape[2]
    tap_count = chirp.shape[1]
    next_rim = from_behind(signal[:, :, :tap_count], "rng", -1)
    extended = jnp.concatenate([signal, next_rim], axis=2)
    block_count = range_count // CBLK
    extra_blocks = tap_count // CBLK
    blocks = extended.reshape(2, pulse_count, block_count + extra_blocks, CBLK)
    blocks = jnp.transpose(blocks, (1, 2, 0, 3)).reshape(
        pulse_count, block_count + extra_blocks, 2 * CBLK
    )
    parts_table = lag_tables(chirp, extra_blocks)
    chirp_real = parts_table[0]
    chirp_imag = parts_table[1]
    upper_rows = jnp.concatenate([chirp_real, -chirp_imag], axis=2)
    lower_rows = jnp.concatenate([chirp_imag, chirp_real], axis=2)
    tables = jnp.concatenate([upper_rows, lower_rows], axis=1)

    def add_piece(lag, accumulated):
        window = lax.dynamic_slice_in_dim(blocks, lag, block_count, 1)
        table = lax.dynamic_index_in_dim(tables, lag, 0, keepdims=False)
        return accumulated + jnp.einsum(
            "pbi,io->pbo", window, table, preferred_element_type=jnp.float32
        )

    accumulated = lax.fori_loop(
        0, extra_blocks + 1, add_piece, jnp.zeros((pulse_count, block_count, 2 * CBLK), jnp.float32)
    )
    accumulated = accumulated.reshape(pulse_count, block_count, 2, CBLK)
    return (
        jnp.transpose(accumulated, (2, 0, 1, 3))
        .reshape(2, pulse_count, range_count)
        .astype(jnp.bfloat16)
    )


def on_device(echoes, chirp, steer, pulse_order, band_coef, band_start, band_width):
    compressed = compress(echoes[:, 0], chirp)
    pulse_rows = lax.all_to_all(compressed, "section", split_axis=2, concat_axis=1, tiled=True)
    position_count = pulse_order.shape[1]
    positions = jnp.arange(position_count, dtype=jnp.int32)
    selector = (positions[:, None] == pulse_order[0][None, :]).astype(jnp.bfloat16)
    weights = jnp.einsum(
        "sqj,jk->sqk", steer[:, 0], selector, preferred_element_type=jnp.float32
    ).astype(jnp.bfloat16)
    forming = jnp.concatenate(
        [
            jnp.concatenate([weights[0], -weights[1]], axis=1),
            jnp.concatenate([weights[1], weights[0]], axis=1),
        ],
        axis=0,
    )
    stacked_rows = jnp.concatenate([pulse_rows[0], pulse_rows[1]], axis=0)
    beam_count = weights.shape[1]
    level_image = (
        jnp.dot(forming, stacked_rows, preferred_element_type=jnp.float32)
        .reshape(2, beam_count, pulse_rows.shape[2])
        .astype(jnp.bfloat16)
    )
    bit_count = lax.axis_size("sub").bit_length() - 1
    coef_all = band_coef[:, 0]
    start_all = band_start[:, 0]
    width_all = band_width[:, 0]
    section_count = coef_all.shape[0]
    for level in range(section_count):
        partner_image = from_partner(level_image, "sub", level % bit_count)
        level_image = merge_level(
            level_image, partner_image, coef_all[level], start_all[level], width_all[level]
        )
    return level_image[:, :, None, :]


def solution(mesh):
    return jax.shard_map(
        on_device,
        mesh=mesh,
        in_specs=(
            P(None, "sub", "section", "rng"),
            P(),
            P(None, "sub", None, None),
            P("sub", None),
            P(None, "sub", None, None, None, None),
            P(None, "sub", None, None),
            P(None, "sub", None, None),
        ),
        out_specs=P(None, "sub", "rng", "section"),
        check_vma=False,
    )
```

profile of v0, /device:TPU:1, one launch (start us, length us, event | category | flops | bytes accessed | tf_op | source)
XLA Modules:
  0.0 180.4 jit_solution(6251457165325808575)
XLA Ops:
  0.0 1.5 slice.437
  1.5 8.8 %collective-permute-start = (bf16[2,6,2048]{2,0,1:T(2,128)(2,1)}, bf16[2,6,2048]{2,0,1:T(2,128)(2,1)}, u32[]{:S(2)}, u32[]{:S(2)}) collective-permute-start(bf16[2,6,2048]{2,0,1:T(2,128)(2,1)} %slice.437), channel_id=1, source_target_pairs={{1,0},{2,1},{3,2},{5,4},{6,5},{7,6},{9,8},{10,9},{11,10},{13,12},{... | collective-permute-start | bytes 147464 | tf_op jit(solution)/shard_map/ppermute | solution.py:12
  11.1 1.3 copy.173
  12.4 0.9 slice.438
  13.3 2.1 %reshape.582 = bf16[622336]{0:T(1024)(128)(2,1)S(1)} reshape(bf16[2,311168]{1,0:T(2,128)(2,1)S(1)} %slice.438) | data formatting | bytes 2489344
  15.5 2.2 %reshape.578 = bf16[2,128,2431]{2,1,0:T(8,128)(2,1)S(1)} reshape(bf16[622336]{0:T(1024)(128)(2,1)S(1)} %reshape.582) | data formatting | bytes 2489344 | tf_op jit(solution)/shard_map/reshape | solution.py:62
  17.7 1.1 slice.439
  18.7 1.7 copy.133
  20.6 0.9 fusion.186
  25.3 0.7 fusion.208
  33.1 0.7 fusion.204
  34.5 0.8 iota_subtract_fusion.6
  35.3 1.4 maximum_maximum_fusion
  36.7 1.1 maximum_bitcast_fusion
  37.9 4.0 %while.14 = (s32[]{:T(128)}, f32[6,32,256]{2,1,0:T(8,128)S(1)}, bf16[6,48,256]{2,1,0:T(8,128)(2,1)S(1)}, bf16[17,256,256]{2,1,0:T(8,128)(2,1)S(1)}, s32[]{:T(128)}, /*index=5*/s32[]{:T(128)}) while((s32[]{:T(128)}, f32[6,32,256]{2,1,0:T(8,128)S(1)}, bf16[6,48,256]{2,1,0:T(8,128)(2,1)S(1)}, bf16[17,256,256]{2,1,0:T(8,128)(2,1)S(1)}, ...), condition=%wide.region_1.2_spmd.clone, body=%wide.region_0.1_spmd.clone.sunk | while | flops 25264132 | bytes 623695 | solution.py:93
  41.9 1.4 copy.140
  43.3 4.2 %reshape.584 = bf16[4,2,6144]{2,1,0:T(2,128)(2,1)} reshape(bf16[4096,2,6]{2,1,0:T(2,128)(2,1)S(1)} %bitcast.228) | data formatting | bytes 196608
  47.5 3.5 %all-to-all-start = ((bf16[4,2,6144]{2,1,0:T(2,128)(2,1)}), bf16[4,2,6144]{2,1,0:T(2,128)(2,1)S(1)}, u32[]{:S(2)}, u32[]{:S(2)}) async-start(bf16[4,2,6144]{2,1,0:T(2,128)(2,1)} %reshape.584), calls=%async_computation | async-start | bytes 196608 | tf_op jit(solution)/shard_map/all_to_all | solution.py:106
  51.0 4.9 %all-to-all-done = bf16[4,2,6144]{2,1,0:T(2,128)(2,1)S(1)} async-done(((bf16[4,2,6144]{2,1,0:T(2,128)(2,1)}), bf16[4,2,6144]{2,1,0:T(2,128)(2,1)S(1)}, u32[]{:S(2)}, u32[]{:S(2)}) %all-to-all-start) | async-done | bytes 98336 | tf_op jit(solution)/shard_map/all_to_all | solution.py:106
  55.9 4.8 %reshape.585 = bf16[4096,2,6]{2,1,0:T(2,128)(2,1)S(1)} reshape(bf16[4,2,6144]{2,1,0:T(2,128)(2,1)S(1)} %all-to-all-done) | data formatting | bytes 196608
  60.7 1.5 copy.141
  62.8 1.9 %collective-permute-start.1 = (bf16[2,128,1024]{2,1,0:T(8,128)(2,1)S(1)}, bf16[2,128,1024]{2,1,0:T(8,128)(2,1)S(1)}, u32[]{:S(2)}, u32[]{:S(2)}) collective-permute-start(bf16[2,128,1024]{2,1,0:T(8,128)(2,1)S(1)} %bitcast.233), channel_id=1, source_target_pairs={{0,4},{4,0},{8,12},{12,8},{16,20},{20,16},{24,28},{28,24},{32,36},... | collective-permute-start | bytes 1572872 | tf_op jit(solution)/shard_map/ppermute | solution.py:22
  65.6 12.2 %collective-permute-done.1 = bf16[2,128,1024]{2,1,0:T(8,128)(2,1)S(1)} collective-permute-done((bf16[2,128,1024]{2,1,0:T(8,128)(2,1)S(1)}, bf16[2,128,1024]{2,1,0:T(8,128)(2,1)S(1)}, u32[]{:S(2)}, u32[]{:S(2)}) %collective-permute-start.1) | collective-permute-done | bytes 524320 | tf_op jit(solution)/shard_map/ppermute | solution.py:22
  78.4 2.1 %collective-permute-start.2 = (bf16[2,128,1024]{2,1,0:T(8,128)(2,1)S(1)}, bf16[2,128,1024]{2,1,0:T(8,128)(2,1)S(1)}, u32[]{:S(2)}, u32[]{:S(2)}) collective-permute-start(bf16[2,128,1024]{2,1,0:T(8,128)(2,1)S(1)} %bitcast.247), channel_id=1, source_target_pairs={{0,8},{8,0},{4,12},{12,4},{16,24},{24,16},{20,28},{28,20},{32,40},... | collective-permute-start | bytes 1572872 | tf_op jit(solution)/shard_map/ppermute | solution.py:22
  81.2 25.1 %collective-permute-done.2 = bf16[2,128,1024]{2,1,0:T(8,128)(2,1)S(1)} collective-permute-done((bf16[2,128,1024]{2,1,0:T(8,128)(2,1)S(1)}, bf16[2,128,1024]{2,1,0:T(8,128)(2,1)S(1)}, u32[]{:S(2)}, u32[]{:S(2)}) %collective-permute-start.2) | collective-permute-done | bytes 524320 | tf_op jit(solution)/shard_map/ppermute | solution.py:22
  107.0 3.0 %collective-permute-start.3 = (bf16[2,128,1024]{2,1,0:T(8,128)(2,1)S(1)}, bf16[2,128,1024]{2,1,0:T(8,128)(2,1)S(1)}, u32[]{:S(2)}, u32[]{:S(2)}) collective-permute-start(bf16[2,128,1024]{2,1,0:T(8,128)(2,1)S(1)} %bitcast.248), channel_id=1, source_target_pairs={{0,16},{16,0},{4,20},{20,4},{8,24},{24,8},{12,28},{28,12},{32,48},... | collective-permute-start | bytes 1572872 | tf_op jit(solution)/shard_map/ppermute | solution.py:22
  110.8 24.9 %collective-permute-done.3 = bf16[2,128,1024]{2,1,0:T(8,128)(2,1)S(1)} collective-permute-done((bf16[2,128,1024]{2,1,0:T(8,128)(2,1)S(1)}, bf16[2,128,1024]{2,1,0:T(8,128)(2,1)S(1)}, u32[]{:S(2)}, u32[]{:S(2)}) %collective-permute-start.3) | collective-permute-done | bytes 524320 | tf_op jit(solution)/shard_map/ppermute | solution.py:22
  136.2 1.9 %collective-permute-start.4 = (bf16[2,128,1024]{2,1,0:T(8,128)(2,1)S(1)}, bf16[2,128,1024]{2,1,0:T(8,128)(2,1)S(1)}, u32[]{:S(2)}, u32[]{:S(2)}) collective-permute-start(bf16[2,128,1024]{2,1,0:T(8,128)(2,1)S(1)} %bitcast.249), channel_id=1, source_target_pairs={{0,32},{32,0},{4,36},{36,4},{8,40},{40,8},{12,44},{44,12},{16,48},... | collective-permute-start | bytes 1572872 | tf_op jit(solution)/shard_map/ppermute | solution.py:22
  138.9 11.9 %collective-permute-done.4 = bf16[2,128,1024]{2,1,0:T(8,128)(2,1)S(1)} collective-permute-done((bf16[2,128,1024]{2,1,0:T(8,128)(2,1)S(1)}, bf16[2,128,1024]{2,1,0:T(8,128)(2,1)S(1)}, u32[]{:S(2)}, u32[]{:S(2)}) %collective-permute-start.4) | collective-permute-done | bytes 524320 | tf_op jit(solution)/shard_map/ppermute | solution.py:22
  151.4 3.2 %collective-permute-start.5 = (bf16[2,128,1024]{2,1,0:T(8,128)(2,1)S(1)}, bf16[2,128,1024]{2,1,0:T(8,128)(2,1)S(1)}, u32[]{:S(2)}, u32[]{:S(2)}) collective-permute-start(bf16[2,128,1024]{2,1,0:T(8,128)(2,1)S(1)} %bitcast.250), channel_id=1, source_target_pairs={{0,64},{64,0},{4,68},{68,4},{8,72},{72,8},{12,76},{76,12},{16,80},... | collective-permute-start | bytes 1572872 | tf_op jit(solution)/shard_map/ppermute | solution.py:22
  154.8 24.4 %collective-permute-done.5 = bf16[2,128,1024]{2,1,0:T(8,128)(2,1)S(1)} collective-permute-done((bf16[2,128,1024]{2,1,0:T(8,128)(2,1)S(1)}, bf16[2,128,1024]{2,1,0:T(8,128)(2,1)S(1)}, u32[]{:S(2)}, u32[]{:S(2)}) %collective-permute-start.5) | collective-permute-done | bytes 524320 | tf_op jit(solution)/shard_map/ppermute | solution.py:22
  179.2 1.2 convolution_convert_fusion
  (176 shorter events, 21.8 us)
Async XLA Ops:
  0.0 26.7 %copy-start = (bf16[2,1,128,24]{2,3,1,0:T(8,128)(2,1)S(1)}, bf16[2,1,128,24]{2,3,1,0:T(8,128)(2,1)}, u32[]{:S(2)}) copy-start(bf16[2,1,128,24]{2,3,1,0:T(8,128)(2,1)} %param.11) | copy-start | bytes 36868
  1.5 35.3 %collective-permute-start = (bf16[2,6,2048]{2,0,1:T(2,128)(2,1)}, bf16[2,6,2048]{2,0,1:T(2,128)(2,1)}, u32[]{:S(2)}, u32[]{:S(2)}) collective-permute-start(bf16[2,6,2048]{2,0,1:T(2,128)(2,1)} %slice.437), channel_id=1, source_target_pairs={{1,0},{2,1},{3,2},{5,4},{6,5},{7,6},{9,8},{10,9},{11,10},{13,12},{... | collective-permute-start | bytes 147464 | tf_op jit(solution)/shard_map/ppermute | solution.py:12
  21.5 5.2 %copy-start.34 = (s32[1,24]{1,0:T(1,128)S(1)}, s32[1,24]{1,0:T(1,128)}, u32[]{:S(2)}) copy-start(s32[1,24]{1,0:T(1,128)} %param.12) | copy-start | bytes 292
  26.9 4.2 %copy-start.23 = (bf16[2,128,24]{1,2,0:T(8,128)(2,1)}, bf16[2,128,24]{1,2,0:T(8,128)(2,1)S(1)}, u32[]{:S(2)}) copy-start(bf16[2,128,24]{1,2,0:T(8,128)(2,1)S(1)} %fusion.14) | copy-start | bytes 36868
  41.9 9.0 %copy-start.24 = (bf16[2,128,24]{1,2,0:T(8,128)(2,1)S(1)}, bf16[2,128,24]{1,2,0:T(8,128)(2,1)}, u32[]{:S(2)}) copy-start(bf16[2,128,24]{1,2,0:T(8,128)(2,1)} %copy-done.23) | copy-start | bytes 36868
  47.5 8.4 %all-to-all-start = ((bf16[4,2,6144]{2,1,0:T(2,128)(2,1)}), bf16[4,2,6144]{2,1,0:T(2,128)(2,1)S(1)}, u32[]{:S(2)}, u32[]{:S(2)}) async-start(bf16[4,2,6144]{2,1,0:T(2,128)(2,1)} %reshape.584), calls=%async_computation | async-start | bytes 196608 | tf_op jit(solution)/shard_map/all_to_all | solution.py:106
  51.0 11.4 %copy-start.25 = (bf16[128,24]{0,1:T(8,128)(2,1)S(1)}, bf16[128,24]{0,1:T(8,128)(2,1)}, u32[]{:S(2)}) copy-start(bf16[128,24]{0,1:T(8,128)(2,1)} %get-tuple-element.172) | copy-start | bytes 18436
  51.0 11.4 %copy-start.26 = (bf16[128,24]{0,1:T(8,128)(2,1)S(1)}, bf16[128,24]{0,1:T(8,128)(2,1)}, u32[]{:S(2)}) copy-start(bf16[128,24]{0,1:T(8,128)(2,1)} %get-tuple-element.173) | copy-start | bytes 18436
  60.6 4.0 %copy-start.32 = (s32[128]{0:T(128)S(1)}, s32[128]{0:T(128)}, u32[]{:S(2)}) copy-start(s32[128]{0:T(128)} %get-tuple-element.179) | copy-start | bytes 1540
  60.7 4.0 %copy-start.33 = (s32[128]{0:T(128)S(1)}, s32[128]{0:T(128)}, u32[]{:S(2)}) copy-start(s32[128]{0:T(128)} %get-tuple-element.180) | copy-start | bytes 1540
  60.7 4.2 %copy-start.2 = (bf16[1,128,128]{2,0,1:T(2,128)(2,1)S(1)}, bf16[1,128,128]{2,0,1:T(2,128)(2,1)}, u32[]{:S(2)}) copy-start(bf16[1,128,128]{2,0,1:T(2,128)(2,1)} %get-tuple-element.171) | copy-start | bytes 98308
  60.7 4.2 %copy-start.10 = (bf16[1,1,1,2,128,16]{4,5,3,2,1,0:T(8,128)(2,1)S(1)}, bf16[1,1,1,2,128,16]{4,5,3,2,1,0:T(8,128)(2,1)}, u32[]{:S(2)}) copy-start(bf16[1,1,1,2,128,16]{4,5,3,2,1,0:T(8,128)(2,1)} %get-tuple-element.149) | copy-start | bytes 24580
  60.7 4.3 %copy-start.6 = (s32[128,128]{1,0:T(8,128)S(1)}, s32[128,128]{1,0:T(8,128)}, u32[]{:S(2)}) copy-start(s32[128,128]{1,0:T(8,128)} %get-tuple-element.201) | copy-start | bytes 196612
  62.2 15.6 %copy-start.15 = (bf16[128,128]{1,0:T(8,128)(2,1)S(1)}, bf16[128,128]{1,0:T(8,128)(2,1)}, u32[]{:S(2)}) copy-start(bf16[128,128]{1,0:T(8,128)(2,1)} %get-tuple-element.124) | copy-start | bytes 98308
  62.2 15.6 %copy-start.16 = (bf16[128,128]{1,0:T(8,128)(2,1)S(1)}, bf16[128,128]{1,0:T(8,128)(2,1)}, u32[]{:S(2)}) copy-start(bf16[128,128]{1,0:T(8,128)(2,1)} %get-tuple-element.125) | copy-start | bytes 98308
  62.2 15.6 %copy-start.21 = (bf16[128,128]{1,0:T(8,128)(2,1)S(1)}, bf16[128,128]{1,0:T(8,128)(2,1)}, u32[]{:S(2)}) copy-start(bf16[128,128]{1,0:T(8,128)(2,1)} %get-tuple-element.126) | copy-start | bytes 98308
  62.3 15.6 %copy-start.22 = (bf16[128,128]{1,0:T(8,128)(2,1)S(1)}, bf16[128,128]{1,0:T(8,128)(2,1)}, u32[]{:S(2)}) copy-start(bf16[128,128]{1,0:T(8,128)(2,1)} %get-tuple-element.127) | copy-start | bytes 98308
  62.8 15.0 %collective-permute-start.1 = (bf16[2,128,1024]{2,1,0:T(8,128)(2,1)S(1)}, bf16[2,128,1024]{2,1,0:T(8,128)(2,1)S(1)}, u32[]{:S(2)}, u32[]{:S(2)}) collective-permute-start(bf16[2,128,1024]{2,1,0:T(8,128)(2,1)S(1)} %bitcast.233), channel_id=1, source_target_pairs={{0,4},{4,0},{8,12},{12,8},{16,20},{20,16},{24,28},{28,24},{32,36},... | collective-permute-start | bytes 1572872 | tf_op jit(solution)/shard_map/ppermute | solution.py:22
  78.3 28.0 %copy-start.13 = (bf16[128,128]{1,0:T(8,128)(2,1)S(1)}, bf16[128,128]{1,0:T(8,128)(2,1)}, u32[]{:S(2)}) copy-start(bf16[128,128]{1,0:T(8,128)(2,1)} %get-tuple-element.120) | copy-start | bytes 98308
  78.4 28.0 %copy-start.14 = (bf16[128,128]{1,0:T(8,128)(2,1)S(1)}, bf16[128,128]{1,0:T(8,128)(2,1)}, u32[]{:S(2)}) copy-start(bf16[128,128]{1,0:T(8,128)(2,1)} %get-tuple-element.121) | copy-start | bytes 98308
  78.4 28.0 %copy-start.19 = (bf16[128,128]{1,0:T(8,128)(2,1)S(1)}, bf16[128,128]{1,0:T(8,128)(2,1)}, u32[]{:S(2)}) copy-start(bf16[128,128]{1,0:T(8,128)(2,1)} %get-tuple-element.122) | copy-start | bytes 98308
  78.4 28.0 %copy-start.20 = (bf16[128,128]{1,0:T(8,128)(2,1)S(1)}, bf16[128,128]{1,0:T(8,128)(2,1)}, u32[]{:S(2)}) copy-start(bf16[128,128]{1,0:T(8,128)(2,1)} %get-tuple-element.123) | copy-start | bytes 98308
  78.4 28.0 %collective-permute-start.2 = (bf16[2,128,1024]{2,1,0:T(8,128)(2,1)S(1)}, bf16[2,128,1024]{2,1,0:T(8,128)(2,1)S(1)}, u32[]{:S(2)}, u32[]{:S(2)}) collective-permute-start(bf16[2,128,1024]{2,1,0:T(8,128)(2,1)S(1)} %bitcast.247), channel_id=1, source_target_pairs={{0,8},{8,0},{4,12},{12,4},{16,24},{24,16},{20,28},{28,20},{32,40},... | collective-permute-start | bytes 1572872 | tf_op jit(solution)/shard_map/ppermute | solution.py:22
  106.4 3.6 %copy-start.1 = (bf16[1,128,128]{2,0,1:T(2,128)(2,1)S(1)}, bf16[1,128,128]{2,0,1:T(2,128)(2,1)}, u32[]{:S(2)}) copy-start(bf16[1,128,128]{2,0,1:T(2,128)(2,1)} %get-tuple-element.163) | copy-start | bytes 98308
  106.4 3.6 %copy-start.8 = (bf16[1,1,1,2,128,16]{4,5,3,2,1,0:T(8,128)(2,1)S(1)}, bf16[1,1,1,2,128,16]{4,5,3,2,1,0:T(8,128)(2,1)}, u32[]{:S(2)}) copy-start(bf16[1,1,1,2,128,16]{4,5,3,2,1,0:T(8,128)(2,1)} %get-tuple-element.142) | copy-start | bytes 24580
  106.9 28.8 %copy-start.11 = (bf16[128,128]{1,0:T(8,128)(2,1)S(1)}, bf16[128,128]{1,0:T(8,128)(2,1)}, u32[]{:S(2)}) copy-start(bf16[128,128]{1,0:T(8,128)(2,1)} %get-tuple-element.116) | copy-start | bytes 98308
  106.9 28.8 %copy-start.12 = (bf16[128,128]{1,0:T(8,128)(2,1)S(1)}, bf16[128,128]{1,0:T(8,128)(2,1)}, u32[]{:S(2)}) copy-start(bf16[128,128]{1,0:T(8,128)(2,1)} %get-tuple-element.117) | copy-start | bytes 98308
  106.9 28.8 %copy-start.17 = (bf16[128,128]{1,0:T(8,128)(2,1)S(1)}, bf16[128,128]{1,0:T(8,128)(2,1)}, u32[]{:S(2)}) copy-start(bf16[128,128]{1,0:T(8,128)(2,1)} %get-tuple-element.118) | copy-start | bytes 98308
  106.9 28.8 %copy-start.18 = (bf16[128,128]{1,0:T(8,128)(2,1)S(1)}, bf16[128,128]{1,0:T(8,128)(2,1)}, u32[]{:S(2)}) copy-start(bf16[128,128]{1,0:T(8,128)(2,1)} %get-tuple-element.119) | copy-start | bytes 98308
  107.0 28.7 %collective-permute-start.3 = (bf16[2,128,1024]{2,1,0:T(8,128)(2,1)S(1)}, bf16[2,128,1024]{2,1,0:T(8,128)(2,1)S(1)}, u32[]{:S(2)}, u32[]{:S(2)}) collective-permute-start(bf16[2,128,1024]{2,1,0:T(8,128)(2,1)S(1)} %bitcast.248), channel_id=1, source_target_pairs={{0,16},{16,0},{4,20},{20,4},{8,24},{24,8},{12,28},{28,12},{32,48},... | collective-permute-start | bytes 1572872 | tf_op jit(solution)/shard_map/ppermute | solution.py:22
  136.2 14.6 %collective-permute-start.4 = (bf16[2,128,1024]{2,1,0:T(8,128)(2,1)S(1)}, bf16[2,128,1024]{2,1,0:T(8,128)(2,1)S(1)}, u32[]{:S(2)}, u32[]{:S(2)}) collective-permute-start(bf16[2,128,1024]{2,1,0:T(8,128)(2,1)S(1)} %bitcast.249), channel_id=1, source_target_pairs={{0,32},{32,0},{4,36},{36,4},{8,40},{40,8},{12,44},{44,12},{16,48},... | collective-permute-start | bytes 1572872 | tf_op jit(solution)/shard_map/ppermute | solution.py:22
  151.4 27.8 %collective-permute-start.5 = (bf16[2,128,1024]{2,1,0:T(8,128)(2,1)S(1)}, bf16[2,128,1024]{2,1,0:T(8,128)(2,1)S(1)}, u32[]{:S(2)}, u32[]{:S(2)}) collective-permute-start(bf16[2,128,1024]{2,1,0:T(8,128)(2,1)S(1)} %bitcast.250), channel_id=1, source_target_pairs={{0,64},{64,0},{4,68},{68,4},{8,72},{72,8},{12,76},{76,12},{16,80},... | collective-permute-start | bytes 1572872 | tf_op jit(solution)/shard_map/ppermute | solution.py:22
  (10 other events, 24.4 us)
where the time goes:
time: 181 us; the launch traced here: 180 us
  waiting for transfers between devices  103 us (57%)
  local copies, waits for them, and re-layouts  29.8 us (16%)
  starting transfers between devices  24.3 us (13%)
  matrix products  11.7 us (6%)
  other arithmetic  9.67 us (5%)
    ppermute x5, waiting for transfers between devices, from_partner(): return lax.ppermute(block, axis, route)  98.5 us
    unnamed x95, local copies, waits for them, and re-layouts  13.9 us
    ppermute x5, starting transfers between devices, from_partner(): return lax.ppermute(block, axis, route)  12.1 us
    ppermute x1, starting transfers between devices, from_behind(): return lax.ppermute(value, axis, pairs)  8.78 us
    all_to_all x1, waiting for transfers between devices, on_device(): lax.all_to_all(compressed, 'section', split_axis=2, concat_axis=1, tiled=...  4.89 us
    dot_general x10, matrix products, band_matrix(): jnp.einsum('sqt,tqc->sqc', coef_side, selector, preferred_element_type=jn...  4.58 us
  transfers between devices with their start and end apart: 7, of which 6 were waited for; matrix products, arithmetic and copies ran while one was open for 16% of the time, Pallas kernels for 0%

commit v1 on v0

--- a/solution.py
+++ b/solution.py
@@ -103,7 +103,12 @@
 
 def on_device(echoes, chirp, steer, pulse_order, band_coef, band_start, band_width):
     compressed = compress(echoes[:, 0], chirp)
-    pulse_rows = lax.all_to_all(compressed, "section", split_axis=2, concat_axis=1, tiled=True)
+    pulse_rows = jnp.concatenate(
+        lax.all_to_all(
+            jnp.stack(jnp.split(compressed, lax.axis_size("section"), axis=2)), "section", 0, 0
+        ),
+        axis=1,
+    )
     position_count = pulse_order.shape[1]
     positions = jnp.arange(position_count, dtype=jnp.int32)
     selector = (positions[:, None] == pulse_order[0][None, :]).astype(jnp.bfloat16)

time: 181 us -> 171 us (0.945)
  local copies, waits for them, and re-layouts: 29.8 us -> 18.5 us
    unnamed x95 -> x93, local copies, waits for them, and re-layouts: 13.9 us -> 4.97 us
  transfers between devices with their start and end apart: 7 -> 7, of which waited for: 6 -> 6; matrix products, arithmetic and copies ran while one was open for 16% -> 17% of each run, Pallas kernels for 0% -> 0%
where the time goes in v1:
time: 171 us; the launch traced here: 170 us
  waiting for transfers between devices  103 us (60%)
  starting transfers between devices  24.5 us (14%)
  local copies, waits for them, and re-layouts  18.5 us (11%)
  matrix products  11.7 us (7%)
  other arithmetic  10.5 us (6%)
    ppermute x5, waiting for transfers between devices, from_partner(): return lax.ppermute(block, axis, route)  98.4 us
    ppermute x5, starting transfers between devices, from_partner(): return lax.ppermute(block, axis, route)  12.1 us
    ppermute x1, starting transfers between devices, from_behind(): return lax.ppermute(value, axis, pairs)  8.78 us
    unnamed x93, local copies, waits for them, and re-layouts  4.97 us
    all_to_all x1, waiting for transfers between devices, on_device(): lax.all_to_all(jnp.stack(jnp.split(compressed, lax.axis_size('section'),...  4.92 us
    dot_general x10, matrix products, band_matrix(): jnp.einsum('sqt,tqc->sqc', coef_side, selector, preferred_element_type=jn...  4.58 us
    all_to_all x1, starting transfers between devices, on_device(): lax.all_to_all(jnp.stack(jnp.split(compressed, lax.axis_size('section'),...  3.63 us
    dot_general x17, matrix products, add_piece(): jnp.einsum('pbi,io->pbo', window, table, preferred_element_type=jnp.float32)  3.56 us
  transfers between devices with their start and end apart: 7, of which 6 were waited for; matrix products, arithmetic and copies ran while one was open for 17% of the time, Pallas kernels for 0%

profile of v1, /device:TPU:1, one launch (start us, length us, event | category | flops | bytes accessed | tf_op | source)
XLA Modules:
  0.0 169.9 jit_solution(12096952095010586408)
XLA Ops:
  0.0 1.5 slice.437
  1.5 8.8 %collective-permute-start = (bf16[2,6,2048]{2,0,1:T(2,128)(2,1)}, bf16[2,6,2048]{2,0,1:T(2,128)(2,1)}, u32[]{:S(2)}, u32[]{:S(2)}) collective-permute-start(bf16[2,6,2048]{2,0,1:T(2,128)(2,1)} %slice.437), channel_id=1, source_target_pairs={{1,0},{2,1},{3,2},{5,4},{6,5},{7,6},{9,8},{10,9},{11,10},{13,12},{... | collective-permute-start | bytes 147464 | tf_op jit(solution)/shard_map/ppermute | solution.py:12
  10.3 0.7 maximum_maximum_fusion.1
  11.1 1.3 copy.129
  12.4 0.9 slice.438
  13.3 2.1 %reshape.589 = bf16[622336]{0:T(1024)(128)(2,1)S(1)} reshape(bf16[2,311168]{1,0:T(2,128)(2,1)S(1)} %slice.438) | data formatting | bytes 2489344
  15.5 2.2 %reshape.582 = bf16[2,128,2431]{2,1,0:T(8,128)(2,1)S(1)} reshape(bf16[622336]{0:T(1024)(128)(2,1)S(1)} %reshape.589) | data formatting | bytes 2489344 | tf_op jit(solution)/shard_map/reshape | solution.py:62
  17.7 1.1 slice.439
  18.7 1.7 copy.93
  20.6 0.9 fusion.186
  26.2 0.7 fusion.207
  29.7 0.7 fusion.205
  33.2 0.7 fusion.203
  33.9 0.7 fusion.192
  34.6 0.8 iota_subtract_fusion.6
  35.3 1.4 maximum_maximum_fusion
  36.8 1.1 maximum_bitcast_fusion
  38.0 4.0 %while.14 = (s32[]{:T(128)}, f32[6,32,256]{2,1,0:T(8,128)S(1)}, bf16[6,48,256]{2,1,0:T(8,128)(2,1)S(1)}, bf16[17,256,256]{2,1,0:T(8,128)(2,1)S(1)}, s32[]{:T(128)}, /*index=5*/s32[]{:T(128)}) while((s32[]{:T(128)}, f32[6,32,256]{2,1,0:T(8,128)S(1)}, bf16[6,48,256]{2,1,0:T(8,128)(2,1)S(1)}, bf16[17,256,256]{2,1,0:T(8,128)(2,1)S(1)}, ...), condition=%wide.region_1.2_spmd.clone, body=%wide.region_0.1_spmd.clone.sunk | while | flops 25264132 | bytes 623695 | solution.py:93
  42.2 0.8 pad_maximum_fusion
  43.0 3.6 %all-to-all-start = ((bf16[4,2,6,1024]{3,1,2,0:T(2,128)(2,1)}), bf16[4,2,6,1024]{3,1,2,0:T(2,128)(2,1)S(1)}, u32[]{:S(2)}, u32[]{:S(2)}) async-start(bf16[4,2,6,1024]{3,1,2,0:T(2,128)(2,1)} %pad_maximum_fusion), calls=%async_computation | async-start | bytes 196608 | tf_op jit(solution)/shard_map/all_to_all | solution.py:107
  46.6 4.9 %all-to-all-done = bf16[4,2,6,1024]{3,1,2,0:T(2,128)(2,1)S(1)} async-done(((bf16[4,2,6,1024]{3,1,2,0:T(2,128)(2,1)}), bf16[4,2,6,1024]{3,1,2,0:T(2,128)(2,1)S(1)}, u32[]{:S(2)}, u32[]{:S(2)}) %all-to-all-start) | async-done | bytes 98336 | tf_op jit(solution)/shard_map/all_to_all | solution.py:107
  52.4 1.9 %collective-permute-start.1 = (bf16[2,128,1024]{2,1,0:T(8,128)(2,1)S(1)}, bf16[2,128,1024]{2,1,0:T(8,128)(2,1)S(1)}, u32[]{:S(2)}, u32[]{:S(2)}) collective-permute-start(bf16[2,128,1024]{2,1,0:T(8,128)(2,1)S(1)} %bitcast.240), channel_id=1, source_target_pairs={{0,4},{4,0},{8,12},{12,8},{16,20},{20,16},{24,28},{28,24},{32,36},... | collective-permute-start | bytes 1572872 | tf_op jit(solution)/shard_map/ppermute | solution.py:22
  55.2 12.2 %collective-permute-done.1 = bf16[2,128,1024]{2,1,0:T(8,128)(2,1)S(1)} collective-permute-done((bf16[2,128,1024]{2,1,0:T(8,128)(2,1)S(1)}, bf16[2,128,1024]{2,1,0:T(8,128)(2,1)S(1)}, u32[]{:S(2)}, u32[]{:S(2)}) %collective-permute-start.1) | collective-permute-done | bytes 524320 | tf_op jit(solution)/shard_map/ppermute | solution.py:22
  68.0 2.1 %collective-permute-start.2 = (bf16[2,128,1024]{2,1,0:T(8,128)(2,1)S(1)}, bf16[2,128,1024]{2,1,0:T(8,128)(2,1)S(1)}, u32[]{:S(2)}, u32[]{:S(2)}) collective-permute-start(bf16[2,128,1024]{2,1,0:T(8,128)(2,1)S(1)} %bitcast.253), channel_id=1, source_target_pairs={{0,8},{8,0},{4,12},{12,4},{16,24},{24,16},{20,28},{28,20},{32,40},... | collective-permute-start | bytes 1572872 | tf_op jit(solution)/shard_map/ppermute | solution.py:22
  70.9 25.1 %collective-permute-done.2 = bf16[2,128,1024]{2,1,0:T(8,128)(2,1)S(1)} collective-permute-done((bf16[2,128,1024]{2,1,0:T(8,128)(2,1)S(1)}, bf16[2,128,1024]{2,1,0:T(8,128)(2,1)S(1)}, u32[]{:S(2)}, u32[]{:S(2)}) %collective-permute-start.2) | collective-permute-done | bytes 524320 | tf_op jit(solution)/shard_map/ppermute | solution.py:22
  96.6 2.9 %collective-permute-start.3 = (bf16[2,128,1024]{2,1,0:T(8,128)(2,1)S(1)}, bf16[2,128,1024]{2,1,0:T(8,128)(2,1)S(1)}, u32[]{:S(2)}, u32[]{:S(2)}) collective-permute-start(bf16[2,128,1024]{2,1,0:T(8,128)(2,1)S(1)} %bitcast.254), channel_id=1, source_target_pairs={{0,16},{16,0},{4,20},{20,4},{8,24},{24,8},{12,28},{28,12},{32,48},... | collective-permute-start | bytes 1572872 | tf_op jit(solution)/shard_map/ppermute | solution.py:22
  100.4 24.9 %collective-permute-done.3 = bf16[2,128,1024]{2,1,0:T(8,128)(2,1)S(1)} collective-permute-done((bf16[2,128,1024]{2,1,0:T(8,128)(2,1)S(1)}, bf16[2,128,1024]{2,1,0:T(8,128)(2,1)S(1)}, u32[]{:S(2)}, u32[]{:S(2)}) %collective-permute-start.3) | collective-permute-done | bytes 524320 | tf_op jit(solution)/shard_map/ppermute | solution.py:22
  125.8 1.9 %collective-permute-start.4 = (bf16[2,128,1024]{2,1,0:T(8,128)(2,1)S(1)}, bf16[2,128,1024]{2,1,0:T(8,128)(2,1)S(1)}, u32[]{:S(2)}, u32[]{:S(2)}) collective-permute-start(bf16[2,128,1024]{2,1,0:T(8,128)(2,1)S(1)} %bitcast.255), channel_id=1, source_target_pairs={{0,32},{32,0},{4,36},{36,4},{8,40},{40,8},{12,44},{44,12},{16,48},... | collective-permute-start | bytes 1572872 | tf_op jit(solution)/shard_map/ppermute | solution.py:22
  128.4 11.9 %collective-permute-done.4 = bf16[2,128,1024]{2,1,0:T(8,128)(2,1)S(1)} collective-permute-done((bf16[2,128,1024]{2,1,0:T(8,128)(2,1)S(1)}, bf16[2,128,1024]{2,1,0:T(8,128)(2,1)S(1)}, u32[]{:S(2)}, u32[]{:S(2)}) %collective-permute-start.4) | collective-permute-done | bytes 524320 | tf_op jit(solution)/shard_map/ppermute | solution.py:22
  140.8 3.3 %collective-permute-start.5 = (bf16[2,128,1024]{2,1,0:T(8,128)(2,1)S(1)}, bf16[2,128,1024]{2,1,0:T(8,128)(2,1)S(1)}, u32[]{:S(2)}, u32[]{:S(2)}) collective-permute-start(bf16[2,128,1024]{2,1,0:T(8,128)(2,1)S(1)} %bitcast.256), channel_id=1, source_target_pairs={{0,64},{64,0},{4,68},{68,4},{8,72},{72,8},{12,76},{76,12},{16,80},... | collective-permute-start | bytes 1572872 | tf_op jit(solution)/shard_map/ppermute | solution.py:22
  144.3 24.3 %collective-permute-done.5 = bf16[2,128,1024]{2,1,0:T(8,128)(2,1)S(1)} collective-permute-done((bf16[2,128,1024]{2,1,0:T(8,128)(2,1)S(1)}, bf16[2,128,1024]{2,1,0:T(8,128)(2,1)S(1)}, u32[]{:S(2)}, u32[]{:S(2)}) %collective-permute-start.5) | collective-permute-done | bytes 524320 | tf_op jit(solution)/shard_map/ppermute | solution.py:22
  168.7 1.2 convolution_convert_fusion
  (173 shorter events, 20.2 us)
Async XLA Ops:
  0.0 21.5 %copy-start = (bf16[2,1,128,24]{2,3,1,0:T(8,128)(2,1)S(1)}, bf16[2,1,128,24]{2,3,1,0:T(8,128)(2,1)}, u32[]{:S(2)}) copy-start(bf16[2,1,128,24]{2,3,1,0:T(8,128)(2,1)} %param.11) | copy-start | bytes 36868
  1.5 35.3 %collective-permute-start = (bf16[2,6,2048]{2,0,1:T(2,128)(2,1)}, bf16[2,6,2048]{2,0,1:T(2,128)(2,1)}, u32[]{:S(2)}, u32[]{:S(2)}) collective-permute-start(bf16[2,6,2048]{2,0,1:T(2,128)(2,1)} %slice.437), channel_id=1, source_target_pairs={{1,0},{2,1},{3,2},{5,4},{6,5},{7,6},{9,8},{10,9},{11,10},{13,12},{... | collective-permute-start | bytes 147464 | tf_op jit(solution)/shard_map/ppermute | solution.py:12
  20.5 3.0 %copy-start.4 = (bf16[5,1,2,2,128,16]{4,5,3,2,1,0:T(8,128)(2,1)S(1)}, bf16[5,1,2,2,128,16]{4,5,3,2,1,0:T(8,128)(2,1)}, u32[]{:S(2)}) copy-start(bf16[5,1,2,2,128,16]{4,5,3,2,1,0:T(8,128)(2,1)} %param.13) | copy-start | bytes 245764
  38.0 8.7 %copy-start.24 = (bf16[2,128,24]{1,2,0:T(8,128)(2,1)S(1)}, bf16[2,128,24]{1,2,0:T(8,128)(2,1)}, u32[]{:S(2)}) copy-start(bf16[2,128,24]{1,2,0:T(8,128)(2,1)} %copy-done.23) | copy-start | bytes 36868
  38.0 14.1 %copy-start.25 = (bf16[128,24]{0,1:T(8,128)(2,1)S(1)}, bf16[128,24]{0,1:T(8,128)(2,1)}, u32[]{:S(2)}) copy-start(bf16[128,24]{0,1:T(8,128)(2,1)} %get-tuple-element.176) | copy-start | bytes 18436
  38.0 14.1 %copy-start.26 = (bf16[128,24]{0,1:T(8,128)(2,1)S(1)}, bf16[128,24]{0,1:T(8,128)(2,1)}, u32[]{:S(2)}) copy-start(bf16[128,24]{0,1:T(8,128)(2,1)} %get-tuple-element.177) | copy-start | bytes 18436
  38.0 16.4 %copy-start.3 = (bf16[1,128,128]{2,0,1:T(2,128)(2,1)S(1)}, bf16[1,128,128]{2,0,1:T(2,128)(2,1)}, u32[]{:S(2)}) copy-start(bf16[1,128,128]{2,0,1:T(2,128)(2,1)} %get-tuple-element.175) | copy-start | bytes 98308
  42.0 12.3 %copy-start.32 = (s32[128]{0:T(128)S(1)}, s32[128]{0:T(128)}, u32[]{:S(2)}) copy-start(s32[128]{0:T(128)} %get-tuple-element.183) | copy-start | bytes 1540
  42.0 12.3 %copy-start.33 = (s32[128]{0:T(128)S(1)}, s32[128]{0:T(128)}, u32[]{:S(2)}) copy-start(s32[128]{0:T(128)} %get-tuple-element.184) | copy-start | bytes 1540
  42.0 12.5 %copy-start.10 = (bf16[1,1,1,2,128,16]{4,5,3,2,1,0:T(8,128)(2,1)S(1)}, bf16[1,1,1,2,128,16]{4,5,3,2,1,0:T(8,128)(2,1)}, u32[]{:S(2)}) copy-start(bf16[1,1,1,2,128,16]{4,5,3,2,1,0:T(8,128)(2,1)} %get-tuple-element.153) | copy-start | bytes 24580
  42.0 12.6 %copy-start.6 = (s32[128,128]{1,0:T(8,128)S(1)}, s32[128,128]{1,0:T(8,128)}, u32[]{:S(2)}) copy-start(s32[128,128]{1,0:T(8,128)} %get-tuple-element.205) | copy-start | bytes 196612
  43.0 24.5 %copy-start.15 = (bf16[128,128]{1,0:T(8,128)(2,1)S(1)}, bf16[128,128]{1,0:T(8,128)(2,1)}, u32[]{:S(2)}) copy-start(bf16[128,128]{1,0:T(8,128)(2,1)} %get-tuple-element.126) | copy-start | bytes 98308
  43.0 24.5 %copy-start.16 = (bf16[128,128]{1,0:T(8,128)(2,1)S(1)}, bf16[128,128]{1,0:T(8,128)(2,1)}, u32[]{:S(2)}) copy-start(bf16[128,128]{1,0:T(8,128)(2,1)} %get-tuple-element.127) | copy-start | bytes 98308
  43.0 24.5 %copy-start.21 = (bf16[128,128]{1,0:T(8,128)(2,1)S(1)}, bf16[128,128]{1,0:T(8,128)(2,1)}, u32[]{:S(2)}) copy-start(bf16[128,128]{1,0:T(8,128)(2,1)} %get-tuple-element.128) | copy-start | bytes 98308
  43.0 24.5 %copy-start.22 = (bf16[128,128]{1,0:T(8,128)(2,1)S(1)}, bf16[128,128]{1,0:T(8,128)(2,1)}, u32[]{:S(2)}) copy-start(bf16[128,128]{1,0:T(8,128)(2,1)} %get-tuple-element.129) | copy-start | bytes 98308
  43.0 8.6 %all-to-all-start = ((bf16[4,2,6,1024]{3,1,2,0:T(2,128)(2,1)}), bf16[4,2,6,1024]{3,1,2,0:T(2,128)(2,1)S(1)}, u32[]{:S(2)}, u32[]{:S(2)}) async-start(bf16[4,2,6,1024]{3,1,2,0:T(2,128)(2,1)} %pad_maximum_fusion), calls=%async_computation | async-start | bytes 196608 | tf_op jit(solution)/shard_map/all_to_all | solution.py:107
  52.4 15.0 %collective-permute-start.1 = (bf16[2,128,1024]{2,1,0:T(8,128)(2,1)S(1)}, bf16[2,128,1024]{2,1,0:T(8,128)(2,1)S(1)}, u32[]{:S(2)}, u32[]{:S(2)}) collective-permute-start(bf16[2,128,1024]{2,1,0:T(8,128)(2,1)S(1)} %bitcast.240), channel_id=1, source_target_pairs={{0,4},{4,0},{8,12},{12,8},{16,20},{20,16},{24,28},{28,24},{32,36},... | collective-permute-start | bytes 1572872 | tf_op jit(solution)/shard_map/ppermute | solution.py:22
  68.0 28.0 %copy-start.13 = (bf16[128,128]{1,0:T(8,128)(2,1)S(1)}, bf16[128,128]{1,0:T(8,128)(2,1)}, u32[]{:S(2)}) copy-start(bf16[128,128]{1,0:T(8,128)(2,1)} %get-tuple-element.122) | copy-start | bytes 98308
  68.0 28.0 %copy-start.14 = (bf16[128,128]{1,0:T(8,128)(2,1)S(1)}, bf16[128,128]{1,0:T(8,128)(2,1)}, u32[]{:S(2)}) copy-start(bf16[128,128]{1,0:T(8,128)(2,1)} %get-tuple-element.123) | copy-start | bytes 98308
  68.0 28.0 %copy-start.19 = (bf16[128,128]{1,0:T(8,128)(2,1)S(1)}, bf16[128,128]{1,0:T(8,128)(2,1)}, u32[]{:S(2)}) copy-start(bf16[128,128]{1,0:T(8,128)(2,1)} %get-tuple-element.124) | copy-start | bytes 98308
  68.0 28.0 %copy-start.20 = (bf16[128,128]{1,0:T(8,128)(2,1)S(1)}, bf16[128,128]{1,0:T(8,128)(2,1)}, u32[]{:S(2)}) copy-start(bf16[128,128]{1,0:T(8,128)(2,1)} %get-tuple-element.125) | copy-start | bytes 98308
  68.0 28.0 %collective-permute-start.2 = (bf16[2,128,1024]{2,1,0:T(8,128)(2,1)S(1)}, bf16[2,128,1024]{2,1,0:T(8,128)(2,1)S(1)}, u32[]{:S(2)}, u32[]{:S(2)}) collective-permute-start(bf16[2,128,1024]{2,1,0:T(8,128)(2,1)S(1)} %bitcast.253), channel_id=1, source_target_pairs={{0,8},{8,0},{4,12},{12,4},{16,24},{24,16},{20,28},{28,20},{32,40},... | collective-permute-start | bytes 1572872 | tf_op jit(solution)/shard_map/ppermute | solution.py:22
  96.0 3.5 %copy-start.29 = (s32[128]{0:T(128)S(1)}, s32[128]{0:T(128)}, u32[]{:S(2)}) copy-start(s32[128]{0:T(128)} %get-tuple-element.185) | copy-start | bytes 1540
  96.0 3.6 %copy-start.1 = (bf16[1,128,128]{2,0,1:T(2,128)(2,1)S(1)}, bf16[1,128,128]{2,0,1:T(2,128)(2,1)}, u32[]{:S(2)}) copy-start(bf16[1,128,128]{2,0,1:T(2,128)(2,1)} %get-tuple-element.167) | copy-start | bytes 98308
  96.1 3.6 %copy-start.8 = (bf16[1,1,1,2,128,16]{4,5,3,2,1,0:T(8,128)(2,1)S(1)}, bf16[1,1,1,2,128,16]{4,5,3,2,1,0:T(8,128)(2,1)}, u32[]{:S(2)}) copy-start(bf16[1,1,1,2,128,16]{4,5,3,2,1,0:T(8,128)(2,1)} %get-tuple-element.146) | copy-start | bytes 24580
  96.5 28.7 %copy-start.11 = (bf16[128,128]{1,0:T(8,128)(2,1)S(1)}, bf16[128,128]{1,0:T(8,128)(2,1)}, u32[]{:S(2)}) copy-start(bf16[128,128]{1,0:T(8,128)(2,1)} %get-tuple-element.118) | copy-start | bytes 98308
  96.5 28.7 %copy-start.12 = (bf16[128,128]{1,0:T(8,128)(2,1)S(1)}, bf16[128,128]{1,0:T(8,128)(2,1)}, u32[]{:S(2)}) copy-start(bf16[128,128]{1,0:T(8,128)(2,1)} %get-tuple-element.119) | copy-start | bytes 98308
  96.5 28.7 %copy-start.17 = (bf16[128,128]{1,0:T(8,128)(2,1)S(1)}, bf16[128,128]{1,0:T(8,128)(2,1)}, u32[]{:S(2)}) copy-start(bf16[128,128]{1,0:T(8,128)(2,1)} %get-tuple-element.120) | copy-start | bytes 98308
  96.6 28.7 %copy-start.18 = (bf16[128,128]{1,0:T(8,128)(2,1)S(1)}, bf16[128,128]{1,0:T(8,128)(2,1)}, u32[]{:S(2)}) copy-start(bf16[128,128]{1,0:T(8,128)(2,1)} %get-tuple-element.121) | copy-start | bytes 98308
  96.6 28.6 %collective-permute-start.3 = (bf16[2,128,1024]{2,1,0:T(8,128)(2,1)S(1)}, bf16[2,128,1024]{2,1,0:T(8,128)(2,1)S(1)}, u32[]{:S(2)}, u32[]{:S(2)}) collective-permute-start(bf16[2,128,1024]{2,1,0:T(8,128)(2,1)S(1)} %bitcast.254), channel_id=1, source_target_pairs={{0,16},{16,0},{4,20},{20,4},{8,24},{24,8},{12,28},{28,12},{32,48},... | collective-permute-start | bytes 1572872 | tf_op jit(solution)/shard_map/ppermute | solution.py:22
  125.8 14.6 %collective-permute-start.4 = (bf16[2,128,1024]{2,1,0:T(8,128)(2,1)S(1)}, bf16[2,128,1024]{2,1,0:T(8,128)(2,1)S(1)}, u32[]{:S(2)}, u32[]{:S(2)}) collective-permute-start(bf16[2,128,1024]{2,1,0:T(8,128)(2,1)S(1)} %bitcast.255), channel_id=1, source_target_pairs={{0,32},{32,0},{4,36},{36,4},{8,40},{40,8},{12,44},{44,12},{16,48},... | collective-permute-start | bytes 1572872 | tf_op jit(solution)/shard_map/ppermute | solution.py:22
  140.8 27.8 %collective-permute-start.5 = (bf16[2,128,1024]{2,1,0:T(8,128)(2,1)S(1)}, bf16[2,128,1024]{2,1,0:T(8,128)(2,1)S(1)}, u32[]{:S(2)}, u32[]{:S(2)}) collective-permute-start(bf16[2,128,1024]{2,1,0:T(8,128)(2,1)S(1)} %bitcast.256), channel_id=1, source_target_pairs={{0,64},{64,0},{4,68},{68,4},{8,72},{72,8},{12,76},{76,12},{16,80},... | collective-permute-start | bytes 1572872 | tf_op jit(solution)/shard_map/ppermute | solution.py:22
  (10 other events, 24.0 us)
